TPU v7x, 512 devices: a whole 4x4x16 slice. The times are simulated.
512 devices in a mesh: ctx: 64 (over z, x_lo, core), ch: 8 (over x_hi, y).
Axes of the slice: x: 4 (x_hi: 2, x_lo: 2; x = x_hi * 2 + x_lo), y: 4, z: 16, core: 2. Of those that a mesh axis runs over, the one named last changes fastest.
Arguments:
- q_in: bfloat16 [8192, 8192], P('ctx', 'ch'), may hold values from -6 to 6
- k_in: bfloat16 [8192, 8192], P('ctx', 'ch'), may hold values from -6 to 6
- v_in: bfloat16 [8192, 8192], P('ctx', 'ch'), may hold values from -6 to 6
- stretch_of_slot: int32 [128], replicated, may hold values from 0 to 127, each once
- short_weight: float32 [3, 7, 8192], P(None, None, 'ch'), may hold values from -2 to 2
- rates: float32 [16, 8192], P(None, 'ch'), may hold values from 1.2207031e-06 to 0.03
- residues: float32 [16, 8192], P(None, 'ch'), may hold values from -12 to 12
- skip: float32 [8192], P('ch'), may hold values from -4 to 4
- gain: float32 [8192], P('ch'), may hold values from 0.5 to 1.5
Outputs:
- operator_out: bfloat16 [8192, 8192], P('ctx', 'ch')
Inputs may be any that keep to these rules, and one draw needn't show every extreme that they name: stretch_of_slot names every sequence stretch exactly once.
All inputs are finite; a program needn't handle non-finite values.
Results may differ from a plain program's by a relative error of at most 0.001.
Values may be sent and summed in bfloat16 or wider, within the bound.
A program may use at most 64 MiB of HBM per device.

v0:
```python
import jax
import jax.numpy as jnp
from jax import lax
from jax.sharding import PartitionSpec as P

D = 8192


def decay_combine(earlier, later):
    return (earlier[0] * later[0], earlier[1] * later[0] + later[1])


def on_device(q_in, k_in, v_in, stretch_of_slot, short_weight, rates, residues, skip, gain):
    tokens, width = q_in.shape
    stretch = tokens // 2
    reach = short_weight.shape[1] - 1
    order = rates.shape[0]
    span = float(stretch)
    my_index = lax.axis_index("ctx")
    own_stretches = lax.dynamic_slice_in_dim(stretch_of_slot, 2 * my_index, 2)
    stacked = jnp.stack([q_in, k_in, v_in]).reshape(3, 2, stretch, width)
    tail_rows = (
        stacked[:, :, stretch - reach :, :].transpose(1, 0, 2, 3).reshape(2, 3 * reach, width)
    )
    stretch_ids = stretch_of_slot
    select = (stretch_ids[None, :] == own_stretches[:, None] - 1).astype(jnp.bfloat16)
    previous = jnp.einsum(
        "mn,nxw->mxw",
        select,
        lax.all_gather(tail_rows, "ctx", axis=0, tiled=True),
        preferred_element_type=jnp.float32,
    )
    previous = previous.reshape(2, 3, reach, width).transpose(1, 0, 2, 3)
    extended = jnp.concatenate([previous, stacked.astype(jnp.float32)], axis=2)
    features = jnp.zeros((3, 2, stretch, width), jnp.float32)
    for shift_by in range(reach + 1):
        features = (
            features
            + short_weight[:, shift_by][:, None, None, :]
            * extended[:, :, reach - shift_by : reach - shift_by + stretch, :]
        )
    query = features[0]
    mixed_in = features[1] * features[2]
    positions = jnp.arange(stretch, dtype=jnp.float32)
    scaled = residues * jnp.sqrt(-jnp.expm1(-2.0 * rates))

    def mode_pass(mode, state):
        local_conv, ends = state
        rate = lax.dynamic_index_in_dim(rates, mode, 0, keepdims=False)
        amount = lax.dynamic_index_in_dim(scaled, mode, 0, keepdims=False)
        factors = jnp.broadcast_to(jnp.exp(-rate)[None, None, :], mixed_in.shape)
        running = lax.associative_scan(decay_combine, (factors, mixed_in), axis=1)[1]
        local_conv = local_conv + amount[None, None, :] * running
        ends = lax.dynamic_update_index_in_dim(ends, running[:, stretch - 1 : stretch, :], mode, 1)
        return (local_conv, ends)

    local_conv, ends = lax.fori_loop(
        0,
        order,
        mode_pass,
        (jnp.zeros((2, stretch, width), jnp.float32), jnp.zeros((2, order, width), jnp.float32)),
    )
    pieces = lax.all_gather(ends, "ctx", axis=0, tiled=True)
    stretch_ids = stretch_of_slot

    def one_target(target):
        gaps = target - 1 - stretch_ids
        before = gaps >= 0
        steps_back = jnp.maximum(gaps, 0).astype(jnp.float32)
        weights = jnp.where(
            before[:, None, None], jnp.exp(-rates[None] * (span * steps_back[:, None, None])), 0.0
        )
        return jnp.sum(weights * pieces, axis=0)

    starts = lax.map(one_target, own_stretches)

    def carry_pass(mode, total):
        rate = lax.dynamic_index_in_dim(rates, mode, 0, keepdims=False)
        amount = lax.dynamic_index_in_dim(scaled, mode, 0, keepdims=False)
        lifted = jnp.exp(-rate[None, :] * (positions[:, None] + 1.0))
        begin = lax.dynamic_index_in_dim(starts, mode, 1, keepdims=False)
        return total + (amount[None, :] * lifted)[None] * begin[:, None, :]

    carried = lax.fori_loop(0, order, carry_pass, jnp.zeros((2, stretch, width), jnp.float32))
    output = local_conv + carried + skip[None, None, :] * mixed_in
    zvalues = query * output
    squares = lax.psum(jnp.sum(zvalues * zvalues, axis=-1), "ch")
    scale = lax.rsqrt(squares / D + 1e-05)
    normed = (zvalues * scale[:, :, None] * gain[None, None, :]).astype(jnp.bfloat16)
    return normed.reshape(tokens, width)


def solution(mesh):
    in_specs = (
        P("ctx", "ch"),
        P("ctx", "ch"),
        P("ctx", "ch"),
        P(),
        P(None, None, "ch"),
        P(None, "ch"),
        P(None, "ch"),
        P("ch"),
        P("ch"),
    )
    out_specs = P("ctx", "ch")
    return jax.shard_map(
        on_device, mesh=mesh, in_specs=in_specs, out_specs=out_specs, check_vma=False
    )
```

profile of v0, /device:TPU:32, one launch (start us, length us, event | category | flops | bytes accessed | tf_op | source)
XLA Modules:
  0.0 368.7 jit_solution(7288362771378136959)
XLA Ops:
  6.5 1.3 pad_maximum_fusion.6
  8.0 0.7 copy.21
  9.0 130.6 %all-gather.3.cloned.1.call-done = bf16[128,18,1024]{2,1,0:T(8,128)(2,1)} async-done(((bf16[2,18,1024]{2,1,0:T(8,128)(2,1)}), bf16[128,18,1024]{2,1,0:T(8,128)(2,1)}) %all-gather.3.cloned.1.call-update) | async-done | bytes 4718608 | tf_op jit(solution)/shard_map/all_gather | solution.py:30
  139.6 7.8 %fusion.8 = f32[2,18,1024]{2,0,1:T(2,128)S(1)} fusion(bf16[128,18,1024]{2,1,0:T(8,128)(2,1)} %all-gather.3.cloned.1.call-done, s32[128]{0:T(128)S(1)} %copy-done.8, s32[2]{0:T(128)S(1)} %get-tuple-element.404), kind=kOutput, calls=%fused_computation.44 | convolution fusion | flops 9437440 | bytes 4866568 | tf_op jit(solution)/shard_map/mn,nxw->mxw/dot_general | solution.py:27
  147.5 1.4 fusion.13
  148.9 1.2 copy-done
  150.2 43.7 %while.43 = (s32[]{:T(128)}, f32[2,64,1024]{2,1,0:T(8,128)S(1)}, f32[2,16,1024]{2,1,0:T(8,128)S(1)}, f32[16,1024]{1,0:T(8,128)S(1)}, f32[2,64,1024]{2,1,0:T(8,12...) while((s32[]{:T(128)}, f32[2,64,1024]{2,1,0:T(8,128)S(1)}, ...), condition=%wide.region_1.2_spmd.clone, body=%wide.region_0.1_spmd.clone.sunk | while | flops 1394691 | bytes 14254231 | solution.py:57
  152.6 0.3 select_add_fusion.4
  155.4 0.3 select_add_fusion.4
  158.1 0.3 select_add_fusion.4
  160.8 0.3 select_add_fusion.4
  163.6 0.3 select_add_fusion.4
  166.3 0.3 select_add_fusion.4
  169.0 0.3 select_add_fusion.4
  171.8 0.3 select_add_fusion.4
  174.5 0.3 select_add_fusion.4
  177.2 0.3 select_add_fusion.4
  180.0 0.3 select_add_fusion.4
  185.4 0.3 select_add_fusion.4
  188.2 0.3 select_add_fusion.4
  190.9 0.3 select_add_fusion.4
  193.6 0.3 select_add_fusion.4
  194.0 0.6 copy-done.2
  194.6 124.3 %all-gather.5.cloned.1.call-done = f32[128,16,1024]{2,1,0:T(8,128)} async-done(((f32[2,16,1024]{2,1,0:T(8,128)}), f32[128,16,1024]{2,1,0:T(8,128)}) %all-gather.5.cloned.1.call-update) | async-done | bytes 8388624 | tf_op jit(solution)/shard_map/all_gather | solution.py:63
  318.9 11.6 %while.42 = (s32[]{:T(128)}, f32[2,16,1024]{2,1,0:T(8,128)S(1)}, s32[2]{0:T(128)S(1)}, s32[128]{0:T(128)S(1)}, f32[1,16,1024]{2,1,0:T(8,128)S(1)}, /*index=5*/f32[128,16,1024]{2,1,0:T(8,128)}, s32[]{:T(128)}, s32[1]{0:T(128)}) while((s32[]{:T(128)}, f32[2,16,1024]{2,1,0:T(8,128)S(1)}, s32[2]{0:T(128)S(1)}, s32[128]{0:T(128)S(1)}, ...), condition=%wide.region_4.5_spmd, body=%wide.region_2.4_spmd.sunk | while | flops 8372995 | bytes 8653177 | solution.py:75
  318.9 0.6 dynamic_slice.66
  320.2 4.5 %multiply_reduce_fusion.3 = f32[16,1024]{1,0:T(8,128)S(1)} fusion(f32[128,16,1024]{2,1,0:T(8,128)} %get-tuple-element.615, f32[128]{0:T(128)S(1)} %convert_multiply_fusion.2, f32[16,1024]{1,0:T(8,128)S(1)} %bitcast.67, pred[128]{0:T(512)(128)(4,1)S(1)} %subtract_compare_fusion.2), kind=kLoop, calls=%fused_computation.1.clone.1 | loop fusion | flops 8372224 | bytes 8520320 | tf_op jit(solution)/shard_map/while/body/eval_jaxpr/reduce_sum | solution.py:73
  324.7 0.6 dynamic_slice.66
  326.0 4.5 %multiply_reduce_fusion.3 = f32[16,1024]{1,0:T(8,128)S(1)} fusion(f32[128,16,1024]{2,1,0:T(8,128)} %get-tuple-element.615, f32[128]{0:T(128)S(1)} %convert_multiply_fusion.2, f32[16,1024]{1,0:T(8,128)S(1)} %bitcast.67, pred[128]{0:T(512)(128)(4,1)S(1)} %subtract_compare_fusion.2), kind=kLoop, calls=%fused_computation.1.clone.1 | loop fusion | flops 8372224 | bytes 8520320 | tf_op jit(solution)/shard_map/while/body/eval_jaxpr/reduce_sum | solution.py:73
  330.5 6.2 %while.44 = (s32[]{:T(128)}, f32[2,64,1024]{2,1,0:T(8,128)S(1)}, f32[16,1024]{1,0:T(8,128)S(1)}, f32[16,1024]{1,0:T(8,128)S(1)}, f32[2,16,1024]{2,1,0:T(8,128)S(1)}, /*index=5*/s32[]{:T(128)}, s32[]{:T(128)}) while((s32[]{:T(128)}, f32[2,64,1024]{2,1,0:T(8,128)S(1)}, f32[16,1024]{1,0:T(8,128)S(1)}, f32[16,1024]{1,0:T(8,128)S(1)}, ...), condition=%wide.region_6.7_spmd.clone, body=%wide.region_5.6_spmd.clone.sunk | while | flops 525379 | bytes 1639007 | solution.py:84
  336.9 24.1 %psum.7 = f32[2,64]{1,0:T(2,128)S(1)} all-reduce(f32[2,64]{1,0:T(2,128)S(1)} %get-tuple-element.402), channel_id=1, replica_groups=mesh['ctx'=64,'ch'=8] {'ch'}, use_global_device_ids=true, to_apply=%region_8.9 | all-reduce | flops 128 | bytes 1024 | tf_op jit(solution)/shard_map/psum | solution.py:87
  361.0 0.8 multiply_convert_fusion
  (988 shorter events, 39.5 us)
Async XLA Ops:
  6.5 133.1 %all-gather.3.cloned.1.call-start = ((), (), s32[]{:S(2)}) async-start(), calls=%async_computation | async-start | bytes 6389760 | tf_op jit(solution)/shard_map/all_gather | solution.py:30
  6.5 2.2 copy-start.4
  6.5 2.3 copy-start.8
  6.5 2.4 copy-start.3
  6.5 2.4 copy-start.5
  8.7 310.2 %all-gather.5.cloned.1.call-start = ((), (), s32[]{:S(2)}) async-start(), calls=%async_computation.1 | async-start | bytes 8519680 | tf_op jit(solution)/shard_map/all_gather | solution.py:63
  148.9 1.2 copy-start
  193.9 0.7 copy-start.2
  330.5 6.2 %copy-start.1 = (f32[3,2,64,1024]{3,2,1,0:T(8,128)S(1)}, f32[3,2,64,1024]{3,2,1,0:T(8,128)}, u32[]{:S(2)}) copy-start(f32[3,2,64,1024]{3,2,1,0:T(8,128)} %copy-done) | copy-start | bytes 4718596
  330.5 6.2 %copy-start.6 = (f32[1024]{0:T(1024)S(1)}, f32[1024]{0:T(1024)}, u32[]{:S(2)}) copy-start(f32[1024]{0:T(1024)} %param.22) | copy-start | bytes 12292
  336.7 24.3 %copy-start.7 = (f32[1024]{0:T(1024)S(1)}, f32[1024]{0:T(1024)}, u32[]{:S(2)}) copy-start(f32[1024]{0:T(1024)} %param.23) | copy-start | bytes 12292
Sparse Core Ops, SparseCore 0:
  9.5 130.1 all-gather.2
  194.7 124.0 all-gather.4
where the time goes:
time: 369 us
  waiting for transfers between devices  255 us (69%)
  other arithmetic  30.7 us (8%)
  local copies, waits for them, and re-layouts  29.6 us (8%)
  blocking collectives  24.1 us (7%)
  between operations  13.6 us (4%)
  loops' own time  8.04 us (2%)
  matrix products  7.8 us (2%)
    all_gather x1, waiting for transfers between devices, on_device(): lax.all_gather(tail_rows, 'ctx', axis=0, tiled=True)  131 us
    all_gather x1, waiting for transfers between devices, on_device(): pieces = lax.all_gather(ends, 'ctx', axis=0, tiled=True)  124 us
    psum x1, blocking collectives, on_device(): squares = lax.psum(jnp.sum(zvalues * zvalues, axis=-1), 'ch')  24.1 us
    slice x288, local copies, waits for them, and re-layouts, mode_pass(): lax.associative_scan(decay_combine, (factors, mixed_in), axis=1)[1]  13.9 us
    pad x160, local copies, waits for them, and re-layouts, mode_pass(): lax.associative_scan(decay_combine, (factors, mixed_in), axis=1)[1]  9.36 us
    reduce_sum x2, other arithmetic, one_target(): return jnp.sum(weights * pieces, axis=0)  8.94 us
    dot_general x1, matrix products, on_device(): jnp.einsum('mn,nxw->mxw', select, lax.all_gather(tail_rows, 'ctx', axis=0...  7.8 us
  transfers between devices with their start and end apart: 2, of which 2 were waited for; matrix products, arithmetic and copies ran while one was open for 0% of the time, Pallas kernels for 0%

commit v1 on v0

--- a/solution.py
+++ b/solution.py
@@ -11,6 +11,12 @@
 
 
 def on_device(q_in, k_in, v_in, stretch_of_slot, short_weight, rates, residues, skip, gain):
+
+    def _manage_shapes(tile_in, shard_axis="ctx"):
+        a_next = jnp.stack([tile_in for _ in range(lax.axis_size(shard_axis))])
+        base_arr = lax.all_to_all(a_next, axis_name=shard_axis, split_axis=0, concat_axis=0)
+        return jnp.concatenate(base_arr, axis=0)
+
     tokens, width = q_in.shape
     stretch = tokens // 2
     reach = short_weight.shape[1] - 1
@@ -25,10 +31,7 @@
     stretch_ids = stretch_of_slot
     select = (stretch_ids[None, :] == own_stretches[:, None] - 1).astype(jnp.bfloat16)
     previous = jnp.einsum(
-        "mn,nxw->mxw",
-        select,
-        lax.all_gather(tail_rows, "ctx", axis=0, tiled=True),
-        preferred_element_type=jnp.float32,
+        "mn,nxw->mxw", select, _manage_shapes(tail_rows), preferred_element_type=jnp.float32
     )
     previous = previous.reshape(2, 3, reach, width).transpose(1, 0, 2, 3)
     extended = jnp.concatenate([previous, stacked.astype(jnp.float32)], axis=2)

time: 369 us -> 480 us (1.30)
  waiting for transfers between devices: 255 us -> 332 us
  local copies, waits for them, and re-layouts: 29.6 us -> 50.7 us
  starting transfers between devices: 0.04 us -> 17.2 us
    all_to_all x0 -> x1, waiting for transfers between devices: none -> 210 us  [_manage_shapes(): lax.all_to_all(a_next, axis_name=shard_axis, split_axis=0, concat_axis=0)]
    all_gather x1 -> x0, waiting for transfers between devices: 131 us -> none  [on_device(): lax.all_gather(tail_rows, 'ctx', axis=0, tiled=True)]
    all_to_all x0 -> x1, starting transfers between devices: none -> 17 us  [_manage_shapes(): lax.all_to_all(a_next, axis_name=shard_axis, split_axis=0, concat_axis=0)]
    all_to_all x0 -> x1, local copies, waits for them, and re-layouts: none -> 9.11 us  [_manage_shapes(): lax.all_to_all(a_next, axis_name=shard_axis, split_axis=0, concat_axis=0)]
    reshape x2 -> x1, local copies, waits for them, and re-layouts: 0.71 us -> 8.06 us  [_manage_shapes(): return jnp.concatenate(base_arr, axis=0)]
where the time goes in v1:
time: 480 us
  waiting for transfers between devices  332 us (69%)
  local copies, waits for them, and re-layouts  50.7 us (11%)
  other arithmetic  30.6 us (6%)
  blocking collectives  24.1 us (5%)
  starting transfers between devices  17.2 us (4%)
  between operations  13.6 us (3%)
  loops' own time  8.04 us (2%)
    all_to_all x1, waiting for transfers between devices, _manage_shapes(): lax.all_to_all(a_next, axis_name=shard_axis, split_axis=0, concat_axis=0)  210 us
    all_gather x1, waiting for transfers between devices, on_device(): pieces = lax.all_gather(ends, 'ctx', axis=0, tiled=True)  122 us
    psum x1, blocking collectives, on_device(): squares = lax.psum(jnp.sum(zvalues * zvalues, axis=-1), 'ch')  24.1 us
    all_to_all x1, starting transfers between devices, _manage_shapes(): lax.all_to_all(a_next, axis_name=shard_axis, split_axis=0, concat_axis=0)  17 us
    slice x288, local copies, waits for them, and re-layouts, mode_pass(): lax.associative_scan(decay_combine, (factors, mixed_in), axis=1)[1]  13.9 us
  transfers between devices with their start and end apart: 2, of which 2 were waited for; matrix products, arithmetic and copies ran while one was open for 0% of the time, Pallas kernels for 0%

profile of v1, /device:TPU:32, one launch (start us, length us, event | category | flops | bytes accessed | tf_op | source)
XLA Modules:
  0.0 479.8 jit_solution(17824539209110383332)
XLA Ops:
  6.5 1.3 pad_maximum_fusion.6
  7.9 4.6 stack.19
  12.5 17.0 %all-to-all-start = ((bf16[64,2,18,1024]{3,1,2,0:T(2,128)(2,1)}), bf16[64,2,18,1024]{3,1,2,0:T(2,128)(2,1)}, u32[]{:S(2)}, u32[]{:S(2)}) async-start(bf16[64,2,18,1024]{3,1,2,0:T(2,128)(2,1)} %stack.19), calls=%async_computation | async-start | bytes 9437184 | tf_op jit(solution)/shard_map/all_to_all | solution.py:17
  30.1 209.9 %all-to-all-done = bf16[64,2,18,1024]{3,1,2,0:T(2,128)(2,1)} async-done(((bf16[64,2,18,1024]{3,1,2,0:T(2,128)(2,1)}), bf16[64,2,18,1024]{3,1,2,0:T(2,128)(2,1)}, u32[]{:S(2)}, u32[]{:S(2)}) %all-to-all-start) | async-done | bytes 4718624 | tf_op jit(solution)/shard_map/all_to_all | solution.py:17
  240.0 9.1 %copy.17 = bf16[64,2,18,1024]{3,1,0,2:T(2,128)(2,1)} copy(bf16[64,2,18,1024]{3,1,2,0:T(2,128)(2,1)} %all-to-all-done) | data formatting | bytes 9437184 | tf_op jit(solution)/shard_map/all_to_all | solution.py:17
  249.1 8.1 %reshape.121 = bf16[128,18,1024]{2,0,1:T(8,128)(2,1)} reshape(bf16[64,2,18,1024]{3,1,0,2:T(2,128)(2,1)} %copy.17) | data formatting | bytes 9437184 | tf_op jit(solution)/shard_map/reshape | solution.py:18
  257.2 3.1 convolution_bitcast_fusion
  260.4 1.4 fusion.11
  261.8 1.2 copy-done
  263.1 43.7 %while.43 = (s32[]{:T(128)}, f32[2,64,1024]{2,1,0:T(8,128)S(1)}, f32[2,16,1024]{2,1,0:T(8,128)S(1)}, f32[16,1024]{1,0:T(8,128)S(1)}, f32[2,64,1024]{2,1,0:T(8,12...) while((s32[]{:T(128)}, f32[2,64,1024]{2,1,0:T(8,128)S(1)}, ...), condition=%wide.region_1.2_spmd.clone, body=%wide.region_0.1_spmd.clone.sunk | while | flops 1394691 | bytes 14254231 | solution.py:60
  265.5 0.3 select_add_fusion.4
  268.3 0.3 select_add_fusion.4
  271.0 0.3 select_add_fusion.4
  273.7 0.3 select_add_fusion.4
  276.5 0.3 select_add_fusion.4
  279.2 0.3 select_add_fusion.4
  281.9 0.3 select_add_fusion.4
  284.7 0.3 select_add_fusion.4
  298.3 0.3 select_add_fusion.4
  301.1 0.3 select_add_fusion.4
  303.8 0.3 select_add_fusion.4
  306.5 0.3 select_add_fusion.4
  306.9 0.6 copy-done.2
  307.5 122.4 %all-gather.2.cloned.1.call-done = f32[128,16,1024]{2,1,0:T(8,128)} async-done(((f32[2,16,1024]{2,1,0:T(8,128)}), f32[128,16,1024]{2,1,0:T(8,128)}) %all-gather.2.cloned.1.call-update) | async-done | bytes 8388624 | tf_op jit(solution)/shard_map/all_gather | solution.py:66
  430.0 11.6 %while.42 = (s32[]{:T(128)}, f32[2,16,1024]{2,1,0:T(8,128)S(1)}, s32[2]{0:T(128)S(1)}, s32[128]{0:T(128)S(1)}, f32[1,16,1024]{2,1,0:T(8,128)S(1)}, /*index=5*/f32[128,16,1024]{2,1,0:T(8,128)}, s32[]{:T(128)}, s32[1]{0:T(128)}) while((s32[]{:T(128)}, f32[2,16,1024]{2,1,0:T(8,128)S(1)}, s32[2]{0:T(128)S(1)}, s32[128]{0:T(128)S(1)}, ...), condition=%wide.region_4.5_spmd, body=%wide.region_2.4_spmd.sunk | while | flops 8372995 | bytes 8653177 | solution.py:78
  430.0 0.6 dynamic_slice.66
  431.2 4.5 multiply_reduce_fusion.3
  435.8 0.6 dynamic_slice.66
  437.0 4.5 multiply_reduce_fusion.3
  441.5 6.2 %while.44 = (s32[]{:T(128)}, f32[2,64,1024]{2,1,0:T(8,128)S(1)}, f32[16,1024]{1,0:T(8,128)S(1)}, f32[16,1024]{1,0:T(8,128)S(1)}, f32[2,16,1024]{2,1,0:T(8,128)S(1)}, /*index=5*/s32[]{:T(128)}, s32[]{:T(128)}) while((s32[]{:T(128)}, f32[2,64,1024]{2,1,0:T(8,128)S(1)}, f32[16,1024]{1,0:T(8,128)S(1)}, f32[16,1024]{1,0:T(8,128)S(1)}, ...), condition=%wide.region_6.7_spmd.clone, body=%wide.region_5.6_spmd.clone.sunk | while | flops 525379 | bytes 1639007 | solution.py:87
  448.0 24.1 %psum.7 = f32[2,64]{1,0:T(2,128)S(1)} all-reduce(f32[2,64]{1,0:T(2,128)S(1)} %get-tuple-element.397), channel_id=1, replica_groups=mesh['ctx'=64,'ch'=8] {'ch'}, use_global_device_ids=true, to_apply=%region_8.9 | all-reduce | flops 128 | bytes 1024 | tf_op jit(solution)/shard_map/psum | solution.py:90
  472.1 0.8 multiply_convert_fusion
  (989 shorter events, 40.6 us)
Async XLA Ops:
  12.5 17.3 %copy-start.4 = (f32[3,7,1024]{2,1,0:T(8,128)S(1)}, f32[3,7,1024]{2,1,0:T(8,128)}, u32[]{:S(2)}) copy-start(f32[3,7,1024]{2,1,0:T(8,128)} %param.19) | copy-start | bytes 258052
  12.5 17.4 %copy-start.8 = (s32[128]{0:T(128)S(1)}, s32[128]{0:T(128)}, u32[]{:S(2)}) copy-start(s32[128]{0:T(128)} %param.18) | copy-start | bytes 1540
  12.5 17.5 %copy-start.3 = (f32[16,1024]{1,0:T(8,128)S(1)}, f32[16,1024]{1,0:T(8,128)}, u32[]{:S(2)}) copy-start(f32[16,1024]{1,0:T(8,128)} %param.20) | copy-start | bytes 196612
  12.5 17.5 %copy-start.5 = (f32[16,1024]{1,0:T(8,128)S(1)}, f32[16,1024]{1,0:T(8,128)}, u32[]{:S(2)}) copy-start(f32[16,1024]{1,0:T(8,128)} %param.21) | copy-start | bytes 196612
  12.5 227.5 %all-to-all-start = ((bf16[64,2,18,1024]{3,1,2,0:T(2,128)(2,1)}), bf16[64,2,18,1024]{3,1,2,0:T(2,128)(2,1)}, u32[]{:S(2)}, u32[]{:S(2)}) async-start(bf16[64,2,18,1024]{3,1,2,0:T(2,128)(2,1)} %stack.19), calls=%async_computation | async-start | bytes 9437184 | tf_op jit(solution)/shard_map/all_to_all | solution.py:17
  29.5 400.4 %all-gather.2.cloned.1.call-start = ((), (), s32[]{:S(2)}) async-start(), calls=%async_computation.1 | async-start | bytes 8519680 | tf_op jit(solution)/shard_map/all_gather | solution.py:66
  261.8 1.2 copy-start
  306.8 0.7 copy-start.2
  441.5 6.2 %copy-start.1 = (f32[3,2,64,1024]{3,2,1,0:T(8,128)S(1)}, f32[3,2,64,1024]{3,2,1,0:T(8,128)}, u32[]{:S(2)}) copy-start(f32[3,2,64,1024]{3,2,1,0:T(8,128)} %copy-done) | copy-start | bytes 4718596
  441.5 6.2 %copy-start.6 = (f32[1024]{0:T(1024)S(1)}, f32[1024]{0:T(1024)}, u32[]{:S(2)}) copy-start(f32[1024]{0:T(1024)} %param.22) | copy-start | bytes 12292
  447.8 24.3 %copy-start.7 = (f32[1024]{0:T(1024)S(1)}, f32[1024]{0:T(1024)}, u32[]{:S(2)}) copy-start(f32[1024]{0:T(1024)} %param.23) | copy-start | bytes 12292
Sparse Core Ops, SparseCore 0:
  307.6 122.2 all-gather.1
